TPU v7x, 32 devices: a whole 2x2x4 slice. The times are simulated.
32 devices in a mesh: chan: 8 (over z, x), tm: 4 (over y, core).
Axes of the slice: x: 2, y: 2, z: 4, core: 2. Of those that a mesh axis runs over, the one named last changes fastest.
Arguments:
- volts: bfloat16 [8, 64, 2, 98304], P('chan', None, None, 'tm'), may hold values from -6 to 6
- scales: float32 [8, 64, 384], P('chan', None, 'tm'), may hold values from 0.25 to 4
- dm_rate: int32 [8, 16, 2], replicated, may hold values from 8192 to 16384
Outputs:
- dedispersed: bfloat16 [64, 8, 2, 98304], P('chan', None, None, 'tm')
All inputs are finite; a program needn't handle non-finite values.
Results may differ from a plain program's by a relative error of at most 0.0083.
Values may be sent and summed in bfloat16 or wider, within the bound.
A program may use at most 128 MiB of HBM per device.

v0:
```python
import math

import jax
import jax.numpy as jnp
from jax import lax
from jax.sharding import PartitionSpec as P

RADIX_A = 128
RADIX_B = 256
INTERSECTION = 8192


def from_behind(shard, axis, by):
    peers = lax.axis_size(axis)
    pairs = [(i, i + by) for i in range(peers) if 0 <= i + by < peers]
    return lax.ppermute(shard, axis, pairs)


def dft_parts(radix):
    row_index = lax.broadcasted_iota(jnp.int32, (radix, radix), 0)
    col_index = lax.broadcasted_iota(jnp.int32, (radix, radix), 1)
    angle = 2.0 * math.pi / radix * (row_index * col_index % radix).astype(jnp.float32)
    return (jnp.cos(angle).astype(jnp.bfloat16), (-jnp.sin(angle)).astype(jnp.bfloat16))


def twiddle_parts():
    length = RADIX_A * RADIX_B
    row_index = lax.broadcasted_iota(jnp.int32, (RADIX_A, RADIX_B), 0)
    col_index = lax.broadcasted_iota(jnp.int32, (RADIX_A, RADIX_B), 1)
    angle = 2.0 * math.pi / length * (row_index * col_index % length).astype(jnp.float32)
    return (jnp.cos(angle), -jnp.sin(angle))


def chirp_parts(rates):
    length = RADIX_A * RADIX_B
    row_index = lax.broadcasted_iota(jnp.int32, (RADIX_A, RADIX_B), 0)
    col_index = lax.broadcasted_iota(jnp.int32, (RADIX_A, RADIX_B), 1)
    frequency = row_index + RADIX_A * col_index
    distance = jnp.abs((frequency + length // 2) % length - length // 2)
    upper_part = distance // RADIX_B
    lower_part = distance % RADIX_B
    delay_term = (length - frequency * (INTERSECTION // 2) % length) % length
    rate_grid = rates.reshape(-1, 1, 1)
    first_term = rate_grid * upper_part * upper_part % (4 * RADIX_A * RADIX_A)
    second_term = rate_grid * upper_part * lower_part % (2 * RADIX_A * RADIX_A * RADIX_B)
    third_term = rate_grid * lower_part * lower_part
    turns = first_term.astype(jnp.float32) / (4.0 * RADIX_A * RADIX_A)
    turns = turns + second_term.astype(jnp.float32) / (2.0 * RADIX_A * RADIX_A * RADIX_B)
    turns = turns + third_term.astype(jnp.float32) / (4.0 * length * length)
    turns = turns + delay_term.astype(jnp.float32) / (1.0 * length)
    angle = 2.0 * math.pi * turns
    return (jnp.cos(angle), jnp.sin(angle))


def dedisperse(data, prior, rates):
    lead_shape = data.shape[:2]
    streams = data.shape[0] * data.shape[1]
    head_rows = INTERSECTION // RADIX_B
    own_rows = data.reshape(streams, 2, RADIX_A - head_rows, RADIX_B)
    early_rows = prior.reshape(streams, 2, head_rows, RADIX_B)
    left_re, left_im = dft_parts(RADIX_A)
    right_re, right_im = dft_parts(RADIX_B)
    forward_left = jnp.stack(
        [jnp.stack([left_re, -left_im], 1), jnp.stack([left_im, left_re], 1)], 0
    )
    forward_right = jnp.stack(
        [jnp.stack([right_re, right_im], 1), jnp.stack([-right_im, right_re], 1)], 0
    )
    inverse_right = jnp.stack(
        [jnp.stack([right_re, -right_im], 1), jnp.stack([right_im, right_re], 1)], 0
    )
    inverse_left = jnp.stack(
        [jnp.stack([left_re, left_im], 1), jnp.stack([-left_im, left_re], 1)], 0
    )
    joined_rows = jnp.concatenate([early_rows, own_rows], axis=2)
    section_one = jnp.einsum(
        "dkcn,scnb->sdkb", forward_left, joined_rows, preferred_element_type=jnp.float32
    )
    twist_re, twist_im = twiddle_parts()
    turned = jnp.stack(
        [
            section_one[:, 0] * twist_re - section_one[:, 1] * twist_im,
            section_one[:, 0] * twist_im + section_one[:, 1] * twist_re,
        ],
        1,
    ).astype(jnp.bfloat16)
    spectrum = jnp.einsum(
        "scan,cndm->sdam", turned, forward_right, preferred_element_type=jnp.float32
    )
    chirp_re, chirp_im = chirp_parts(rates)
    shaped = jnp.stack(
        [
            spectrum[:, 0] * chirp_re - spectrum[:, 1] * chirp_im,
            spectrum[:, 0] * chirp_im + spectrum[:, 1] * chirp_re,
        ],
        1,
    ).astype(jnp.bfloat16)
    returned = jnp.einsum(
        "scan,cndm->sdam", shaped, inverse_right, preferred_element_type=jnp.float32
    )
    untwisted = jnp.stack(
        [
            returned[:, 0] * twist_re + returned[:, 1] * twist_im,
            returned[:, 1] * twist_re - returned[:, 0] * twist_im,
        ],
        1,
    ).astype(jnp.bfloat16)
    result = jnp.einsum(
        "dkcn,scnb->sdkb",
        inverse_left[:, head_rows:],
        untwisted,
        preferred_element_type=jnp.float32,
    )
    result = result * (1.0 / (RADIX_A * RADIX_B))
    return result.astype(jnp.bfloat16).reshape(lead_shape + (2, -1))


def body(volts, scales, dm_rate):
    lanes = volts.shape[1]
    seg_len = volts.shape[3]
    block_count = scales.shape[2]
    scaled = (
        volts.reshape(1, lanes, 2, block_count, seg_len // block_count).astype(jnp.float32)
        * scales[:, :, None, :, None]
    )
    values = scaled.reshape(volts.shape).astype(jnp.bfloat16)
    rate_table = jnp.repeat(dm_rate.reshape(dm_rate.shape[0], -1), 2, axis=1)
    groups = lax.axis_size("chan")
    turned = lax.all_to_all(
        values.reshape(lanes, 1, 2, seg_len), "chan", split_axis=0, concat_axis=1, tiled=True
    )
    prior = from_behind(turned[:, :, :, seg_len - INTERSECTION :], "tm", 1)
    own_lanes = lanes // groups
    lane_rates = lax.dynamic_slice_in_dim(
        rate_table, lax.axis_index("chan") * own_lanes, own_lanes, 1
    )
    return dedisperse(turned, prior, jnp.transpose(lane_rates))


def solution(mesh):
    return jax.shard_map(
        body,
        mesh=mesh,
        in_specs=(P("chan", None, None, "tm"), P("chan", None, "tm"), P()),
        out_specs=P("chan", None, None, "tm"),
        check_vma=False,
    )
```

profile of v0, /device:TPU:12, one launch (start us, length us, event | category | flops | bytes accessed | tf_op | source)
XLA Modules:
  0.0 303.2 jit_solution(2522544230964683272)
XLA Ops:
  0.0 0.0 slice-start
  0.0 1.8 mul.461
  1.8 0.0 slice-start.1
  1.8 3.6 %copy.45 = f32[8,8,96,256]{3,1,2,0:T(8,128)S(1)} copy(f32[8,8,96,256]{3,2,1,0:T(8,128)S(1)} %bitcast.111) | data formatting | bytes 12582912
  5.4 0.0 slice-done
  5.4 0.0 slice-done.1
  5.4 7.5 %fusion.23 = bf16[64,1,2,24576]{3,2,1,0:T(2,128)(2,1)S(1)} fusion(bf16[1,64,2,24576]{3,2,1,0:T(2,128)(2,1)S(1)} %bitcast.115, f32[64,24576]{1,0:T(8,128)S(1)} %bitcast.112), kind=kLoop, calls=%fused_computation.45 | loop fusion | flops 9437184 | bytes 18874368 | tf_op jit(solution)/shard_map/reshape | solution.py:130
  12.9 143.3 %all_to_all.18 = bf16[64,1,2,24576]{3,2,1,0:T(2,128)(2,1)S(1)} all-to-all(bf16[64,1,2,24576]{3,2,1,0:T(2,128)(2,1)S(1)} %fusion.23), channel_id=1, replica_groups=mesh['chan'=8,'tm'=4] {'chan'}, dimensions={0} | all-to-all | bytes 12582912 | tf_op jit(solution)/shard_map/all_to_all | solution.py:129
  156.2 0.0 copy-start.3
  156.2 3.5 %copy.56 = bf16[8,8,1,2,24576]{4,0,1,3,2:T(8,128)(2,1)S(1)} copy(bf16[8,8,1,2,24576]{4,3,1,0,2:T(2,128)(2,1)S(1)} %bitcast.109) | data formatting | bytes 12582912 | tf_op jit(solution)/shard_map/all_to_all | solution.py:129
  159.7 0.0 copy-start
  159.7 2.7 copy-done
  162.4 1.5 slice.38
  163.9 1.9 collective-permute-start
  165.8 0.0 copy-done.3
  165.8 0.1 copy.25
  165.9 0.1 mul.478
  166.0 0.3 fusion.74
  166.3 0.3 negate_convert_fusion.1
  166.6 1.0 fusion.73
  167.6 0.5 sine_negate_fusion
  168.1 1.3 negate_convert_fusion
  169.4 0.6 fusion.65
  170.0 0.9 fusion.33
  170.9 0.2 fusion.51
  171.1 0.3 add_select_fusion.6
  171.3 7.3 %copy.47 = bf16[16,8,96,256]{3,2,1,0:T(8,128)(2,1)} copy(bf16[16,8,96,256]{3,1,2,0:T(8,128)(2,1)} %bitcast.108) | data formatting | bytes 12582912
  178.6 10.1 %copy.23 = bf16[64,2,96,256]{2,3,1,0:T(8,128)(2,1)} copy(bf16[64,2,96,256]{3,2,0,1:T(8,128)(2,1)} %bitcast.110) | data formatting | bytes 12582912 | tf_op jit(solution)/shard_map/reshape | solution.py:59
  188.8 2.7 collective-permute-done
  191.4 0.0 copy-start.1
  191.4 1.3 copy-done.1
  192.7 2.2 copy.46
  194.9 5.9 %copy.22 = bf16[64,2,32,256]{2,3,1,0:T(8,128)(2,1)} copy(bf16[64,2,32,256]{3,2,0,1:T(8,128)(2,1)S(1)} %bitcast.113) | data formatting | bytes 4194304 | tf_op jit(solution)/shard_map/reshape | solution.py:60
  200.8 16.3 %convolution_bitcast_fusion.1 = f32[64,2,128,256]{2,3,1,0:T(8,128)} fusion(bf16[64,2,96,256]{2,3,1,0:T(8,128)(2,1)} %copy.23, bf16[64,2,32,256]{2,3,1,0:T(8,128)(2,1)} %copy.22, bf16[1,128,2,128]{3,1,2,0:T(8,128)(2,1)S(1)} %get-tuple-element.20, bf16[1,128,2,128]{3,1,2,0:T(8,128)(2,1)S(1)} %get-tuple-element.23), kind=kOutput, calls=%fused_computation.14 | convolution fusion | flops 2164523008 | bytes 25296896 | tf_op jit(solution)/shard_map/dkcn,scnb->sdkb/dot_general | solution.py:76
  217.1 8.7 %subtract_convert_fusion.2 = (bf16[64,1,128,256]{2,3,1,0:T(8,128)(2,1)S(1)}, bf16[64,1,128,256]{2,3,1,0:T(8,128)(2,1)}) fusion(f32[64,2,128,256]{2,3,1,0:T(8,128)} %convolution_bitcast_fusion.1, f32[128,256]{0,1:T(8,128)S(1)} %get-tuple-element.29, f32[128,256]{0,1:T(8,128)S(1)} %get-tuple-element.30), kind=kLoop, calls=%fused_computation.43 | loop fusion | flops 16777216 | bytes 25427968 | tf_op jit(solution)/shard_map/convert.4
  225.9 6.9 %fusion.22 = f32[64,2,128,256]{2,3,0,1:T(8,128)S(1)} fusion(bf16[64,1,128,256]{2,3,1,0:T(8,128)(2,1)} %get-tuple-element.10, bf16[64,1,128,256]{2,3,1,0:T(8,128)(2,1)S(1)} %get-tuple-element.9, bf16[1,256,2,256]{1,3,0,2:T(8,128)(2,1)} %get-tuple-element.14, bf16[1,256,2,256]{1,3,0,2:T(8,128)(2,1)} %get-tuple-element.17), kind=kOutput, calls=%fused_computation.44 | convolution fusion | flops 4312793088 | bytes 25690112 | tf_op jit(solution)/shard_map/scan,cndm->sdam/dot_general | solution.py:87
  232.8 42.3 %subtract_convert_fusion.1 = (bf16[64,1,128,256]{2,3,0,1:T(8,128)(2,1)S(1)}, bf16[64,1,128,256]{2,3,0,1:T(8,128)(2,1)}) fusion(f32[64,2,128,256]{2,3,0,1:T(8,128)S(1)} %fusion.22, f32[128,256]{0,1:T(8,128)S(1)} %fusion.51, s32[128,256]{0,1:T(8,128)S(1)} %get-tuple-element.26, s32[128,256]{0,1:T(8,128)S(1)} %get-tuple-element.25, s32[64]{0:T(128)S(1)} %mul.478), kind=kLoop, calls=%fused_computation.41 | loop fusion | flops 94371840 | bytes 25559296 | tf_op jit(solution)/shard_map/convert.2
  275.1 6.3 %convolution_bitcast_fusion = f32[64,2,128,256]{2,3,1,0:T(8,128)S(1)} fusion(bf16[64,1,128,256]{2,3,0,1:T(8,128)(2,1)} %get-tuple-element.6, bf16[64,1,128,256]{2,3,0,1:T(8,128)(2,1)S(1)} %get-tuple-element.5, bf16[1,256,2,256]{1,3,2,0:T(8,128)(2,1)S(1)} %get-tuple-element.18, bf16[1,256,2,256]{1,3,2,0:T(8,128)(2,1)S(1)} %get-tuple-element.13), kind=kOutput, calls=%fused_computation.13 | convolution fusion | flops 4299423744 | bytes 25690112 | tf_op jit(solution)/shard_map/scan,cndm->sdam/dot_general | solution.py:98
  281.4 0.0 copy-start.2
  281.4 2.5 add_convert_fusion
  283.9 0.0 copy-done.2
  283.9 5.0 %fusion.24 = bf16[64,2,96,256]{3,2,1,0:T(8,128)(2,1)} fusion(bf16[64,1,128,256]{2,3,1,0:T(8,128)(2,1)S(1)} %get-tuple-element.8, bf16[64,1,128,256]{2,3,1,0:T(8,128)(2,1)S(1)} %get-tuple-element.7, bf16[1,128,2,128]{3,1,2,0:T(8,128)(2,1)S(1)} %copy-done.2, bf16[1,128,2,128]{3,1,2,0:T(8,128)(2,1)S(1)} %get-tuple-element.19), kind=kOutput, calls=%fused_computation.46 | convolution fusion | flops 1633878016 | bytes 14811136 | tf_op jit(solution)/shard_map/dkcn,scnb->sdkb/dot_general | solution.py:108
  289.0 14.2 %reshape.446 = bf16[8,8,2,24576]{3,2,1,0:T(2,128)(2,1)} reshape(bf16[64,2,96,256]{3,2,1,0:T(8,128)(2,1)} %fusion.24) | data formatting | bytes 12582912 | tf_op jit(solution)/shard_map/reshape | solution.py:115
  (4 shorter events, 0.0 us)
Async XLA Ops:
  0.0 5.4 %slice-start = ((s8[6291456]{0:T(1024)(128)(4,1)}), s8[4194304]{0:T(1024)(128)(4,1)S(1)}, s32[]{:S(2)}) async-start(s8[6291456]{0:T(1024)(128)(4,1)} %bitcast.114), calls=%async_computation.1 | async-start | bytes 8388608
  1.8 3.6 %slice-start.1 = ((s8[6291456]{0:T(1024)(128)(4,1)}), s8[2097152]{0:T(1024)(128)(4,1)S(1)}, s32[]{:S(2)}) async-start(s8[6291456]{0:T(1024)(128)(4,1)} %bitcast.114), calls=%async_computation.2 | async-start | bytes 4194304
  156.2 9.6 %copy-start.3 = (s32[8,16,2]{1,2,0:T(2,128)S(1)}, s32[8,16,2]{1,2,0:T(2,128)}, u32[]{:S(2)}) copy-start(s32[8,16,2]{1,2,0:T(2,128)} %param.5) | copy-start | bytes 3076
  159.7 2.7 copy-start
  163.9 27.6 %collective-permute-start = (bf16[8,8,2,8192]{3,1,0,2:T(8,128)(2,1)}, bf16[8,8,2,8192]{3,1,0,2:T(8,128)(2,1)S(1)}, u32[]{:S(2)}, u32[]{:S(2)}) collective-permute-start(bf16[8,8,2,8192]{3,1,0,2:T(8,128)(2,1)} %slice.38), channel_id=1, source_target_pairs={{0,1},{1,2},{2,3},{4,5},{5,6},{6,7},{8,9},{9,10},{10,11},{12,13},{... | collective-permute-start | bytes 6291464 | tf_op jit(solution)/shard_map/ppermute | solution.py:16
  191.4 1.3 copy-start.1
  281.4 2.5 copy-start.2
where the time goes:
time: 305 us; the launch traced here: 303 us
  blocking collectives  143 us (47%)
  other arithmetic  66.4 us (22%)
  local copies, waits for them, and re-layouts  54.2 us (18%)
  matrix products  34.6 us (11%)
    all_to_all x1, blocking collectives, body(): lax.all_to_all(values.reshape(lanes, 1, 2, seg_len), 'chan', split_axis=0...  143 us
    another operation x3, other arithmetic  53.5 us
    unnamed x16, local copies, waits for them, and re-layouts  17.2 us
    dot_general x1, matrix products, dedisperse(): jnp.einsum('dkcn,scnb->sdkb', forward_left, joined_rows, preferred_elemen...  16.3 us
    reshape x1, local copies, waits for them, and re-layouts, dedisperse(): return result.astype(jnp.bfloat16).reshape(lead_shape + (2, -1))  14.2 us
    reshape x1, local copies, waits for them, and re-layouts, dedisperse(): own_rows = data.reshape(streams, 2, RADIX_A - head_rows, RADIX_B)  10.1 us
    reshape x1, other arithmetic, body(): values.reshape(lanes, 1, 2, seg_len)  7.53 us
    dot_general x1, matrix products, dedisperse(): jnp.einsum('scan,cndm->sdam', turned, forward_right, preferred_element_ty...  6.9 us
  transfers between devices with their start and end apart: 1, of which 1 were waited for; matrix products, arithmetic and copies ran while one was open for 8% of the time, Pallas kernels for 0%

commit v1 on v0

v1 whole, which is shorter than its diff:
```python
import functools
import math

import jax
import jax.numpy as jnp
import ml_dtypes
import numpy as np
from jax import lax
from jax.experimental import pallas as pl
from jax.experimental.pallas import tpu as pltpu
from jax.sharding import PartitionSpec as P

RADIX_A = 128
RADIX_B = 256
NFFT = RADIX_A * RADIX_B
INTERSECTION = 8192
LANE = 128
HALVES = RADIX_B // LANE
PRIOR = INTERSECTION // LANE * 2
MESH = pl.DeviceIdType.MESH


def dft_parts(radix):
    index = np.arange(radix)
    angle = 2.0 * np.pi / radix * (np.outer(index, index) % radix)
    rounded = lambda x: x.astype(np.float32).astype(ml_dtypes.bfloat16).astype(np.float32)
    return rounded(np.cos(angle)), rounded(-np.sin(angle))


def tables():
    are, aim = dft_parts(RADIX_A)
    bre, bim = dft_parts(RADIX_B)
    eye = np.eye(HALVES, dtype=np.float32)
    left = np.array([[are, -aim], [aim, are]])
    left = np.einsum("dckn,hg->hdkngc", left, eye).reshape(HALVES * 2 * RADIX_A, -1)
    back = np.array([[are, aim], [-aim, are]]) / NFFT
    back = np.einsum("dcnk,hg->nhdgck", back, eye).reshape(-1, HALVES * 2 * RADIX_A)
    back = back[PRIOR:]
    right = np.array([[bre, bim], [-bim, bre]])
    right = right.transpose(0, 2, 1, 3).reshape(2 * RADIX_B, 2 * RADIX_B)
    unright = np.array([[bre, -bim], [bim, bre]])
    unright = unright.transpose(0, 2, 1, 3).reshape(2 * RADIX_B, 2 * RADIX_B)
    turn = np.outer(np.arange(RADIX_A), np.arange(RADIX_B)) % NFFT
    angle = 2.0 * np.pi / NFFT * turn
    twist = np.stack([np.cos(angle), -np.sin(angle)]).astype(np.float32)
    half = lambda x: x.astype(ml_dtypes.bfloat16)
    return half(left), half(right), half(unright), half(back), twist


def chirp(rate):
    shape = (RADIX_A, RADIX_B)
    k = lax.broadcasted_iota(jnp.int32, shape, 0) + RADIX_A * lax.broadcasted_iota(jnp.int32, shape, 1)
    g = jnp.minimum(k, NFFT - k)
    phase = rate * (g * g) - (k << 29)
    quarter = (phase + (1 << 29)) >> 30
    x = (phase - (quarter << 30)).astype(jnp.float32) * (2.0 * math.pi / 2.0**32)
    y = x * x
    s = x + x * y * (-1.6666654611e-1 + y * (8.3321608736e-3 + y * -1.9515295891e-4))
    c = 1.0 + y * (-0.5 + y * (4.166664568298827e-2 + y * (-1.388731625493765e-3 + y * 2.443315711809948e-5)))
    odd = (quarter & 1) == 1
    re = jnp.where(odd, s, c)
    im = jnp.where(odd, c, s)
    re = jnp.where(((quarter + 1) & 2) == 2, -re, re)
    im = jnp.where((quarter & 2) == 2, -im, im)
    return re, im


def bitwise_xor(a, b, bits):
    total = 0
    for i in range(bits):
        total = total + (a // 2**i + b // 2**i) % 2 * 2**i
    return total


def kernel(n, n_tm, own, width, rates, scales, volts, left_in, right_in, unright_in, back_in, twist_in,
           out, values, got, tail, left, right, unright, back, twist, square, spread,
           load_sem, table_sem, send_sem, recv_sem, tail_send, tail_recv):
    me = lax.axis_index("chan")
    tm = lax.axis_index("tm")
    groups = own // width
    items = n * groups
    rows = values.shape[1]
    bits = (n - 1).bit_length()

    def place(i):
        return i // n, bitwise_xor(me, i % n, bits)

    def load(i):
        g, peer = place(i)
        at = pl.ds(peer * own + g * width, width)
        return pltpu.make_async_copy(volts.at[at], values.at[at], load_sem.at[i])

    fills = [
        pltpu.make_async_copy(src, dst, table_sem.at[j])
        for j, (src, dst) in enumerate(
            [(left_in, left), (twist_in, twist), (right_in, right), (unright_in, unright), (back_in, back)]
        )
    ]

    barrier = pltpu.get_barrier_semaphore()

    @pl.loop(1, n)
    def _(r):
        pl.semaphore_signal(barrier, inc=1, device_id={"chan": bitwise_xor(me, r, bits)}, device_id_type=MESH)

    pl.semaphore_signal(barrier, inc=1, device_id={"tm": (tm + n_tm - 1) % n_tm}, device_id_type=MESH)
    pl.semaphore_signal(barrier, inc=1, device_id={"tm": (tm + 1) % n_tm}, device_id_type=MESH)

    @pl.loop(0, items)
    def _(i):
        load(i).start()

    for fill in fills:
        fill.start()

    lanes, count = scales.shape
    square[...] = jnp.zeros_like(square)
    square[0:lanes, 0:count] = scales[...]
    flipped = square[...].T[0:count]
    for j in range(rows // count):
        spread[pl.ds(j, count, stride=rows // count), :] = flipped

    pl.semaphore_wait(barrier, n + 1)

    def exchange(i):
        g, peer = place(i)
        return pltpu.make_async_remote_copy(
            src_ref=values.at[pl.ds(peer * own + g * width, width)],
            dst_ref=got.at[me, pl.ds(g * width, width)],
            send_sem=send_sem.at[i],
            recv_sem=recv_sem.at[i],
            device_id={"chan": peer},
            device_id_type=MESH,
        )

    def forward(i):
        g, peer = place(i)
        return pltpu.make_async_remote_copy(
            src_ref=got.at[peer, pl.ds(g * width, width), pl.ds(rows - PRIOR, PRIOR)],
            dst_ref=tail.at[peer, pl.ds(g * width, width)],
            send_sem=tail_send.at[i],
            recv_sem=tail_recv.at[i],
            device_id={"tm": tm + 1},
            device_id_type=MESH,
        )

    @pl.loop(0, items)
    def _(i):
        g, peer = place(i)
        load(i).wait()
        first = peer * own + g * width
        turned = pltpu.roll(spread[...], (LANE - first) % LANE, 1)
        for s in range(width):
            scale = jnp.broadcast_to(turned[:, s : s + 1], (rows, LANE))
            scaled = (values[first + s].astype(jnp.float32) * scale).astype(jnp.bfloat16)

            @pl.when(i % n > 0)
            def _():
                values[first + s] = scaled

            @pl.when(i % n == 0)
            def _():
                got[me, g * width + s] = scaled

        @pl.when(i % n > 0)
        def _():
            exchange(i).start()

    @pl.when(tm == 0)
    def _():
        @pl.loop(0, n)
        def _(c):
            tail[c] = jnp.zeros(tail.shape[1:], tail.dtype)

    for fill in fills:
        fill.wait()

    def advance(i):
        @pl.when(i % n > 0)
        def _():
            exchange(i).wait_recv()

        @pl.when(tm < n_tm - 1)
        def _():
            forward(i).start()

    advance(0)

    @pl.loop(0, items)
    def _(i):
        @pl.when(i + 1 < items)
        def _():
            advance(i + 1)

        @pl.when(tm > 0)
        def _():
            forward(i).wait_recv()

        g, c = place(i)
        base = g * width
        lane = me * own + base
        rate = rates[c, lane // 2 % 2, lane // 4]
        cre, cim = chirp(rate)
        wre, wim = twist[0], twist[1]
        streams = [
            jnp.concatenate([tail[c, base + s], got[c, base + s]], axis=0) for s in range(width)
        ]
        section = jnp.dot(
            left[...], jnp.concatenate(streams, axis=1), preferred_element_type=jnp.float32
        )
        ups = []
        for s in range(width):
            cols = slice(s * LANE, (s + 1) * LANE)
            part = lambda d: jnp.concatenate(
                [section[(h * 2 + d) * RADIX_A : (h * 2 + d + 1) * RADIX_A, cols] for h in range(HALVES)], axis=1
            )
            sre, sim = part(0), part(1)
            turned = jnp.concatenate(
                [(sre * wre - sim * wim).astype(jnp.bfloat16), (sre * wim + sim * wre).astype(jnp.bfloat16)], axis=1
            )
            spec = jnp.dot(turned, right[...], preferred_element_type=jnp.float32)
            sre, sim = spec[:, :RADIX_B], spec[:, RADIX_B:]
            shaped = jnp.concatenate(
                [(sre * cre - sim * cim).astype(jnp.bfloat16), (sre * cim + sim * cre).astype(jnp.bfloat16)], axis=1
            )
            spun = jnp.dot(shaped, unright[...], preferred_element_type=jnp.float32)
            sre, sim = spun[:, :RADIX_B], spun[:, RADIX_B:]
            ure = (sre * wre + sim * wim).astype(jnp.bfloat16)
            uim = (sim * wre - sre * wim).astype(jnp.bfloat16)
            pieces = []
            for h in range(HALVES):
                pieces += [ure[:, h * LANE : (h + 1) * LANE], uim[:, h * LANE : (h + 1) * LANE]]
            ups.append(jnp.concatenate(pieces, axis=0))
        result = jnp.dot(
            back[...], jnp.concatenate(ups, axis=1), preferred_element_type=jnp.float32
        ).astype(jnp.bfloat16)
        for s in range(width):
            out[base + s, c] = result[:, s * LANE : (s + 1) * LANE]

    @pl.loop(0, items)
    def _(i):
        @pl.when(i % n > 0)
        def _():
            exchange(i).wait_send()

        @pl.when(tm < n_tm - 1)
        def _():
            forward(i).wait_send()


def body(volts, scales, dm_rate):
    lanes, seg_len = volts.shape[1], volts.shape[3]
    count = scales.shape[2]
    n, n_tm = lax.axis_size("chan"), lax.axis_size("tm")
    own = lanes // n
    width = 2 if own % 2 == 0 else 1
    rows = seg_len // LANE * 2
    values = volts.reshape(lanes, 2, seg_len // LANE, LANE).transpose(0, 2, 1, 3).reshape(lanes, rows, LANE)
    left, right, unright, back, twist = tables()
    items = n * (own // width)
    vmem = pl.BlockSpec(memory_space=pltpu.VMEM)
    dma = pltpu.SemaphoreType.DMA
    out = pl.pallas_call(
        functools.partial(kernel, n, n_tm, own, width),
        out_shape=jax.ShapeDtypeStruct((own, n, rows, LANE), jnp.bfloat16),
        in_specs=[pl.BlockSpec(memory_space=pltpu.SMEM), vmem] + [pl.BlockSpec(memory_space=pltpu.MemorySpace.HBM)] * 6,
        out_specs=vmem,
        scratch_shapes=[
            pltpu.VMEM((lanes, rows, LANE), jnp.bfloat16),
            pltpu.VMEM((n, own, rows, LANE), jnp.bfloat16),
            pltpu.VMEM((n, own, PRIOR, LANE), jnp.bfloat16),
        ]
        + [pltpu.VMEM(x.shape, x.dtype) for x in (left, right, unright, back, twist)]
        + [
            pltpu.VMEM((LANE, LANE), jnp.float32),
            pltpu.VMEM((rows, LANE), jnp.float32),
            dma((items,)),
            dma((5,)),
            dma((items,)),
            dma((items,)),
            dma((items,)),
            dma((items,)),
        ],
        compiler_params=pltpu.CompilerParams(
            collective_id=0, has_side_effects=True, vmem_limit_bytes=56 * 2**20
        ),
        name="dedisperse",
    )(dm_rate.transpose(0, 2, 1), scales.reshape(lanes, count), values, left, right, unright, back, twist)
    out = out.reshape(own, n, seg_len // LANE, 2, LANE).transpose(0, 1, 3, 2, 4)
    return out.reshape(own, n, 2, seg_len)


def solution(mesh):
    return jax.shard_map(
        body,
        mesh=mesh,
        in_specs=(P("chan", None, None, "tm"), P("chan", None, "tm"), P()),
        out_specs=P("chan", None, None, "tm"),
        check_vma=False,
    )
```

time: 305 us -> 163 us (0.53)
  Pallas kernels: 0 us -> 155 us
  blocking collectives: 143 us -> 0 us
  other arithmetic: 66.4 us -> 0 us
  local copies, waits for them, and re-layouts: 54.2 us -> 6.88 us
  matrix products: 34.6 us -> 0 us
    pallas_call x0 -> x1, Pallas kernels: none -> 155 us  [body(): pl.pallas_call(functools.partial(kernel, n, n_tm, own, width), out_shape=...]
    all_to_all x1 -> x0, blocking collectives: 143 us -> none  [body(): lax.all_to_all(values.reshape(lanes, 1, 2, seg_len), 'chan', split_axis=0...]
    another operation x5 -> x0, other arithmetic: 55 us -> none
    dot_general x4 -> x0, matrix products: 34.6 us -> none  [the longest x1 16.3 us: dedisperse(): jnp.einsum('dkcn,scnb->sdkb', forward_left, joined_rows, preferred_elemen...]
    reshape x3 -> x0, local copies, waits for them, and re-layouts: 30.2 us -> none  [the longest x1 14.2 us: dedisperse(): return result.astype(jnp.bfloat16).reshape(lead_shape + (2, -1))]
    unnamed x16 -> x1, local copies, waits for them, and re-layouts: 17.2 us -> 6.88 us
    reshape x1 -> x0, other arithmetic: 7.53 us -> none  [body(): values.reshape(lanes, 1, 2, seg_len)]
    all_to_all x1 -> x0, local copies, waits for them, and re-layouts: 3.47 us -> none  [body(): lax.all_to_all(values.reshape(lanes, 1, 2, seg_len), 'chan', split_axis=0...]
  transfers between devices with their start and end apart: 1 -> 0, of which waited for: 1 -> 0; matrix products, arithmetic and copies ran while one was open for 8% -> 0% of each run, Pallas kernels for 0% -> 0%
where the time goes in v1:
time: 163 us; the launch traced here: 162 us
  Pallas kernels  155 us (95%)
  local copies, waits for them, and re-layouts  6.88 us (4%)
    pallas_call x1, Pallas kernels, body(): pl.pallas_call(functools.partial(kernel, n, n_tm, own, width), out_shape=...  155 us
    unnamed x1, local copies, waits for them, and re-layouts  6.88 us

profile of v1, /device:TPU:12, one launch (start us, length us, event | category | flops | bytes accessed | tf_op | source)
XLA Modules:
  0.0 162.3 jit_solution(10290670474132630032)
XLA Ops:
  0.0 155.4 %dedisperse.1 = bf16[8,8,384,128]{3,2,1,0:T(8,128)(2,1)} custom-call(s32[8,2,16]{2,1,0:T(2,128)} %bitcast.15, f32[64,96]{1,0:T(8,128)} %bitcast.14, bf16[64,384,128]{2,1,0:T(8,128)(2,1)} %bitcast.13, bf16[512,512]{1,0:T(8,128)(2,1)} %constant.10.clone.left_in, bf16[512,512]{1,0:T(8,128)(2,1)} %constant.11.clone.right_in, ...), custom_call_target="tpu_custom_call" | custom-call | tf_op jit(solution)/shard_map/dedisperse/pallas_call | solution.py:263
  155.4 6.9 %copy.12 = bf16[8,8,2,24576]{3,2,1,0:T(2,128)(2,1)} copy(bf16[8,8,2,24576]{3,2,1,0:T(2,128)(2,1)} %bitcast.12) | data formatting | bytes 12582912

commit v2 on v1

--- a/solution.py
+++ b/solution.py
@@ -248,6 +248,18 @@
             forward(i).wait_send()
 
 
+def settle(chunks, src, out, out_sem):
+    size = src.shape[0] // chunks
+    copies = [
+        pltpu.make_async_copy(src.at[pl.ds(j * size, size)], out.at[pl.ds(j * size, size)], out_sem.at[j])
+        for j in range(chunks)
+    ]
+    for copy in copies:
+        copy.start()
+    for copy in copies:
+        copy.wait()
+
+
 def body(volts, scales, dm_rate):
     lanes, seg_len = volts.shape[1], volts.shape[3]
     count = scales.shape[2]
@@ -259,11 +271,12 @@
     left, right, unright, back, twist = tables()
     items = n * (own // width)
     vmem = pl.BlockSpec(memory_space=pltpu.VMEM)
+    hbm = pl.BlockSpec(memory_space=pltpu.MemorySpace.HBM)
     dma = pltpu.SemaphoreType.DMA
     out = pl.pallas_call(
         functools.partial(kernel, n, n_tm, own, width),
-        out_shape=jax.ShapeDtypeStruct((own, n, rows, LANE), jnp.bfloat16),
-        in_specs=[pl.BlockSpec(memory_space=pltpu.SMEM), vmem] + [pl.BlockSpec(memory_space=pltpu.MemorySpace.HBM)] * 6,
+        out_shape=pltpu.VMEM((own, n, rows, LANE), jnp.bfloat16),
+        in_specs=[pl.BlockSpec(memory_space=pltpu.SMEM), vmem] + [hbm] * 6,
         out_specs=vmem,
         scratch_shapes=[
             pltpu.VMEM((lanes, rows, LANE), jnp.bfloat16),
@@ -282,10 +295,19 @@
             dma((items,)),
         ],
         compiler_params=pltpu.CompilerParams(
-            collective_id=0, has_side_effects=True, vmem_limit_bytes=56 * 2**20
+            collective_id=0, has_side_effects=True, vmem_limit_bytes=52 * 2**20
         ),
         name="dedisperse",
     )(dm_rate.transpose(0, 2, 1), scales.reshape(lanes, count), values, left, right, unright, back, twist)
+    out = pl.pallas_call(
+        functools.partial(settle, own),
+        out_shape=jax.ShapeDtypeStruct((own * n, rows, LANE), jnp.bfloat16),
+        in_specs=[vmem],
+        out_specs=hbm,
+        scratch_shapes=[dma((own,))],
+        compiler_params=pltpu.CompilerParams(vmem_limit_bytes=16 * 2**20),
+        name="settle",
+    )(out.reshape(own * n, rows, LANE))
     out = out.reshape(own, n, seg_len // LANE, 2, LANE).transpose(0, 1, 3, 2, 4)
     return out.reshape(own, n, 2, seg_len)
 

time: 163 us -> 156 us (0.957)
  local copies, waits for them, and re-layouts: 6.88 us -> 0 us
    unnamed x1 -> x0, local copies, waits for them, and re-layouts: 6.88 us -> none
    pallas_call x0 -> x1, Pallas kernels: none -> 2.74 us  [body(): pl.pallas_call(functools.partial(settle, own), out_shape=jax.ShapeDtypeSt...]
    pallas_call x1, Pallas kernels: 155 us -> 153 us  [body(): pl.pallas_call(functools.partial(kernel, n, n_tm, own, width), out_shape=...]
where the time goes in v2:
time: 156 us
  Pallas kernels  155 us (99%)
    pallas_call x1, Pallas kernels, body(): pl.pallas_call(functools.partial(kernel, n, n_tm, own, width), out_shape=...  153 us

profile of v2, /device:TPU:12, one launch (start us, length us, event | category | flops | bytes accessed | tf_op | source)
XLA Modules:
  0.0 155.5 jit_solution(10029896116667385915)
XLA Ops:
  0.0 152.8 %dedisperse.1 = bf16[8,8,384,128]{3,2,1,0:T(8,128)(2,1)S(1)} custom-call(s32[8,2,16]{2,1,0:T(2,128)} %bitcast.16, f32[64,96]{1,0:T(8,128)} %bitcast.15, bf16[64,384,128]{2,1,0:T(8,128)(2,1)} %bitcast.14, bf16[512,512]{1,0:T(8,128)(2,1)} %constant.10.clone.left_in, bf16[512,512]{1,0:T(8,128)(2,1)} %constant.11.clone.right_in, ...), custom_call_target="tpu_custom_call" | custom-call | tf_op jit(solution)/shard_map/dedisperse/pallas_call | solution.py:276
  152.8 2.7 %settle.1 = bf16[64,384,128]{2,1,0:T(8,128)(2,1)} custom-call(bf16[64,384,128]{2,1,0:T(8,128)(2,1)S(1)} %bitcast.13), custom_call_target="tpu_custom_call" | custom-call | tf_op jit(solution)/shard_map/settle/pallas_call | solution.py:302

commit v3 on v2

--- a/solution.py
+++ b/solution.py
@@ -85,6 +85,10 @@
     def place(i):
         return i // n, bitwise_xor(me, i % n, bits)
 
+    def ahead(j):
+        first = 1 - (j + items - n) // items
+        return j + first * (n - 1 - 2 * j)
+
     def load(i):
         g, peer = place(i)
         at = pl.ds(peer * own + g * width, width)
@@ -107,8 +111,8 @@
     pl.semaphore_signal(barrier, inc=1, device_id={"tm": (tm + 1) % n_tm}, device_id_type=MESH)
 
     @pl.loop(0, items)
-    def _(i):
-        load(i).start()
+    def _(j):
+        load(ahead(j)).start()
 
     for fill in fills:
         fill.start()
@@ -145,7 +149,8 @@
         )
 
     @pl.loop(0, items)
-    def _(i):
+    def _(j):
+        i = ahead(j)
         g, peer = place(i)
         load(i).wait()
         first = peer * own + g * width
@@ -188,19 +193,19 @@
 
     @pl.loop(0, items)
     def _(i):
-        @pl.when(i + 1 < items)
-        def _():
-            advance(i + 1)
-
-        @pl.when(tm > 0)
-        def _():
-            forward(i).wait_recv()
-
         g, c = place(i)
         base = g * width
         lane = me * own + base
-        rate = rates[c, lane // 2 % 2, lane // 4]
-        cre, cim = chirp(rate)
+        cre, cim = chirp(rates[c, lane // 2 % 2, lane // 4])
+
+        @pl.when(i + 1 < items)
+        def _():
+            advance(i + 1)
+
+        @pl.when(tm > 0)
+        def _():
+            forward(i).wait_recv()
+
         wre, wim = twist[0], twist[1]
         streams = [
             jnp.concatenate([tail[c, base + s], got[c, base + s]], axis=0) for s in range(width)

time: 156 us -> 153 us (0.981)
  Pallas kernels: 155 us -> 153 us
    pallas_call x1, Pallas kernels: 153 us -> 150 us  [body(): pl.pallas_call(functools.partial(kernel, n, n_tm, own, width), out_shape=...]
where the time goes in v3:
time: 153 us
  Pallas kernels  153 us (100%)
    pallas_call x1, Pallas kernels, body(): pl.pallas_call(functools.partial(kernel, n, n_tm, own, width), out_shape=...  150 us

profile of v3, /device:TPU:12, one launch (start us, length us, event | category | flops | bytes accessed | tf_op | source)
XLA Modules:
  0.0 152.8 jit_solution(5776627501846700802)
XLA Ops:
  0.0 150.1 %dedisperse.1 = bf16[8,8,384,128]{3,2,1,0:T(8,128)(2,1)S(1)} custom-call(s32[8,2,16]{2,1,0:T(2,128)} %bitcast.16, f32[64,96]{1,0:T(8,128)} %bitcast.15, bf16[64,384,128]{2,1,0:T(8,128)(2,1)} %bitcast.14, bf16[512,512]{1,0:T(8,128)(2,1)} %constant.10.clone.left_in, bf16[512,512]{1,0:T(8,128)(2,1)} %constant.11.clone.right_in, ...), custom_call_target="tpu_custom_call" | custom-call | tf_op jit(solution)/shard_map/dedisperse/pallas_call | solution.py:281
  150.1 2.7 %settle.1 = bf16[64,384,128]{2,1,0:T(8,128)(2,1)} custom-call(bf16[64,384,128]{2,1,0:T(8,128)(2,1)S(1)} %bitcast.13), custom_call_target="tpu_custom_call" | custom-call | tf_op jit(solution)/shard_map/settle/pallas_call | solution.py:307
